TPU v7x, 32 devices: a whole 2x2x4 slice. The times are simulated.
32 devices in a mesh: row: 8 (over z, x), col: 4 (over y, core).
Axes of the slice: x: 2, y: 2, z: 4, core: 2. Of those that a mesh axis runs over, the one named last changes fastest.
Arguments:
- matrix: float32 [8192, 4096], P('row', 'col'), may hold values from -6 to 6
- tile_mask: int32 [64, 32], P('row', 'col'), may hold values 0 or 1
- panel_order: int32 [32], replicated, may hold values from 0 to 31, each once
Outputs:
- factors: float32 [4, 128, 128], replicated
- projections: float32 [4, 128, 4096], P(None, None, 'col')
- remainder: float32 [8192, 4096], P('row', 'col')
Inputs may be any that keep to these rules, and one draw needn't show every extreme that they name: panel_order is a permutation of the column blocks, so the 4 panels differ, and every column block among the first 4 of panel_order has at least one nonzero tile in tile_mask.
All inputs are finite; a program needn't handle non-finite values. No bound on the sum of `tile_mask` on one device may be relied on, other than what follows from the above.
Results may differ from a plain program's by a relative error of at most 0.0001.
Values sent between devices are 32-bit elements; how exact they have to be, the bound alone decides.
No kernel may reach another device: no remote copies, remote signals or barrier semaphores. Data moves between devices by JAX's collectives and lax.ppermute only.
A program may use at most 64 MiB of HBM per device.

v0:
```python
import jax
import jax.numpy as jnp
from jax import lax
from jax.experimental import pallas as pl
from jax.experimental.pallas import tpu as pltpu
from jax.sharding import PartitionSpec as P

PANELS = 4
SUB = 8
HI = lax.Precision.HIGHEST
MID = lax.Precision.HIGH


def swap(x, axis, bit):
    size = lax.axis_size(axis)
    return lax.ppermute(x, axis, [(i, i ^ bit) for i in range(size)])


def bits_of(size):
    return [1 << k for k in range(size.bit_length() - 1)]


def has(axis, bit):
    return (lax.axis_index(axis) // bit) % 2


def after(x, *others):
    return lax.optimization_barrier((x, *others))[0]


def halves(x, b):
    half = x.shape[0] // 2
    return lax.dynamic_slice_in_dim(x, b * half, half, 0), lax.dynamic_slice_in_dim(x, (1 - b) * half, half, 0)


def join(mine, other, b):
    return jnp.where(b == 0, jnp.concatenate([mine, other], 0), jnp.concatenate([other, mine], 0))


def dot_t(a, b, precision=HI):
    return lax.dot_general(a, b, (((0,), (0,)), ((), ())), precision=precision)


def dot_nt(a, b, precision=HI):
    return lax.dot_general(a, b, (((1,), (1,)), ((), ())), precision=precision)


def cut_kernel(order_ref, mask_ref, matrix_ref, out_ref, *, first):
    rows, tile = out_ref.shape
    nb = mask_ref.shape[1]
    b = order_ref[first + pl.program_id(0)]
    mine = jnp.where(b // nb == lax.axis_index("col"), 1.0, 0.0)

    def step(t, carry):
        keep = mine * mask_ref[t, b % nb].astype(jnp.float32)
        s = pl.ds(pl.multiple_of(t * tile, tile), tile)
        out_ref[s, :] = matrix_ref[s, :] * keep
        return carry

    lax.fori_loop(0, rows // tile, step, 0)


def cut_panels(matrix, tile_mask, panel_order, first, count):
    rows, cols = matrix.shape
    nb = tile_mask.shape[1]
    tile = cols // nb
    return pl.pallas_call(
        lambda *refs: cut_kernel(*refs, first=first),
        grid_spec=pltpu.PrefetchScalarGridSpec(
            num_scalar_prefetch=2,
            grid=(count,),
            in_specs=[pl.BlockSpec((rows, tile), lambda p, order, mask: (0, order[first + p] % nb))],
            out_specs=pl.BlockSpec((rows, tile), lambda p, order, mask: (0, p)),
        ),
        out_shape=jax.ShapeDtypeStruct((rows, count * tile), matrix.dtype),
    )(panel_order, tile_mask, matrix)


def eliminate(m_ref, out_ref):
    size, wide = m_ref.shape
    shape = (SUB, wide)
    sub = lax.broadcasted_iota(jnp.int32, shape, 0)
    for r0 in range(0, size, SUB):
        m8 = m_ref[r0 : r0 + SUB, :]
        c = {}
        for j in range(SUB):
            col = jnp.broadcast_to(m8[:, r0 + j : r0 + j + 1], shape)
            for i in range(j, SUB):
                c[i, j] = jnp.broadcast_to(col[i : i + 1, :], shape)
        y = [jnp.broadcast_to(m8[k : k + 1, :], shape) for k in range(SUB)]
        inv, mult = {}, {}
        for k in range(SUB):
            inv[k] = 1.0 / c[k, k]
            for j in range(k + 1, SUB):
                mult[j, k] = c[j, k] * inv[k]
            for j in range(k + 1, SUB):
                for i in range(j, SUB):
                    c[i, j] = c[i, j] - mult[i, k] * c[j, k]
                y[j] = y[j] - mult[j, k] * y[k]
        v = [None] * SUB
        for j in reversed(range(SUB)):
            v[j] = inv[j] * y[j]
            for k in reversed(range(j + 1, SUB)):
                v[j] = v[j] - mult[k, j] * v[k]
        rows, pivots = y[0], c[0, 0]
        for k in range(1, SUB):
            rows = jnp.where(sub == k, y[k], rows)
            pivots = jnp.where(sub == k, c[k, k], pivots)
        out_ref[r0 : r0 + SUB, :] = rows * lax.rsqrt(pivots)
        for t0 in range(r0 + SUB, size, SUB):
            m = m_ref[t0 : t0 + SUB, :]
            left = m
            for j in range(SUB):
                m = m - jnp.broadcast_to(left[:, r0 + j : r0 + j + 1], shape) * v[j]
            m_ref[t0 : t0 + SUB, :] = m


def eliminate_tile(tile_block, m_ref, out_ref, side_ref):
    half = tile_block.shape[0] // 2
    row = lax.broadcasted_iota(jnp.int32, (half, half), 0)
    col = lax.broadcasted_iota(jnp.int32, (half, half), 1)
    unit = jnp.where(row == col, 1.0, 0.0)
    zero = jnp.zeros((half, half), tile_block.dtype)
    m_ref[...] = jnp.concatenate([tile_block[:half, :half], unit], 1)

    def step(h, carry):
        eliminate(m_ref, out_ref.at[h])

        @pl.when(h == 0)
        def _():
            across = jnp.dot(out_ref[0][:, half:], tile_block[:half, half:], precision=HI)
            side_ref[...] = jnp.concatenate([across, across], 1)
            m_ref[...] = jnp.concatenate([tile_block[half:, half:] - dot_t(across, across), unit], 1)

        return carry

    lax.fori_loop(0, 2, step, 0)
    first, second = out_ref[0], out_ref[1]
    v0, v1 = first[:, half:], second[:, half:]
    across = side_ref[:, :half]
    below = -jnp.dot(v1, dot_t(across, v0), precision=HI)
    u0, u1 = (jnp.where(col >= row, x[:, :half], 0.0) for x in (first, second))
    upper = jnp.concatenate([jnp.concatenate([u0, across], 1), jnp.concatenate([zero, u1], 1)], 0)
    inverse = jnp.concatenate([jnp.concatenate([v0, zero], 1), jnp.concatenate([below, v1], 1)], 0)
    return upper, inverse


def factor_kernel(*refs, panel, tile):
    n_in = (2, 2, 4, 5)[panel]
    n_out = (4, 2, 4, 2)[panel]
    ins, outs, (m_ref, both_ref, side_ref, *left) = refs[:n_in], refs[n_in : n_in + n_out], refs[n_in + n_out :]
    if panel % 2 == 0:
        (gram_ref,) = left
        core = lax.axis_index("col") % 2
        half = ins[0].shape[0]
        gram_ref[pl.ds(pl.multiple_of(core * half, half), half), :] = ins[0][...]
        gram_ref[pl.ds(pl.multiple_of((1 - core) * half, half), half), :] = ins[1][...]
    if panel == 0:
        rest, old = gram_ref[...], None
    elif panel == 1:
        rest, old = ins[0][...], ins[1][...]
    elif panel == 2:
        upper, lower = ins[2][...], ins[3][...]
        side = gram_ref[:, : 2 * tile]
        across = jnp.concatenate([dot_nt(upper, side[:, :tile]), dot_nt(lower, side)], 0)
        rest = gram_ref[:, 2 * tile :] - dot_t(across, across)
        old = -jnp.concatenate(
            [dot_t(across[:tile], upper) + dot_t(across[tile:], lower[:, :tile]), dot_t(across[tile:], lower[:, tile:])], 1
        )
    else:
        rest, old = ins[0][...], ins[1][...]
    outs[0][...], v = eliminate_tile(rest[:tile, :tile], m_ref, both_ref, side_ref)
    top = v if old is None else jnp.concatenate([jnp.dot(v, old[:tile], precision=HI), v], 1)
    if panel == 3:
        outs[1][...] = jnp.zeros_like(outs[1])
        for k, done in enumerate(ins[2:]):
            outs[1][k * tile : (k + 1) * tile, : (k + 1) * tile] = done[...]
        outs[1][3 * tile :, :] = top
        return
    outs[1][...] = top
    if panel == 1:
        return
    across = jnp.dot(v, rest[:tile, tile:], precision=HI)
    outs[2][...] = rest[tile:, tile:] - dot_t(across, across)
    below = -dot_t(across, top)
    if old is not None:
        below = below + jnp.concatenate([old[tile:], jnp.zeros((tile, tile), v.dtype)], 1)
    outs[3][...] = below


def factor_step(panel, tile, dtype, *operands):
    f32 = lambda *shape: jax.ShapeDtypeStruct(shape, dtype)
    wide = (panel + 1) * tile
    out = {
        0: (f32(tile, tile), f32(tile, wide), f32(tile, tile), f32(tile, wide)),
        1: (f32(tile, tile), f32(tile, wide)),
        2: (f32(tile, tile), f32(tile, wide), f32(tile, tile), f32(tile, wide)),
        3: (f32(tile, tile), f32(wide, wide)),
    }[panel]
    scratch = [pltpu.VMEM(shape, dtype) for shape in ((tile // 2, tile), (2, tile // 2, tile), (tile // 2, tile))]
    if panel % 2 == 0:
        scratch.append(pltpu.VMEM((2 * tile, (panel + 2) * tile), dtype))
    return pl.pallas_call(
        lambda *refs: factor_kernel(*refs, panel=panel, tile=tile), out_shape=out, scratch_shapes=scratch
    )(*operands)


def on_device(matrix, tile_mask, panel_order):
    rows, cols = matrix.shape
    nb_local = tile_mask.shape[1]
    tile = cols // nb_local
    dtype = matrix.dtype
    order = bits_of(lax.axis_size("row"))
    pair, *others = bits_of(lax.axis_size("col"))
    core = has("col", pair)
    shares = lax.axis_size("col")
    index = core * (shares // 2) + lax.axis_index("col") // 2

    def share_of(gram):
        part = gram.shape[0] // shares
        return lax.dynamic_slice_in_dim(gram, index * part, part, 0)

    def side_by_side(mine, other):
        return jnp.where(core == 0, jnp.concatenate([mine, other], 1), jnp.concatenate([other, mine], 1))

    mine = [cut_panels(matrix, tile_mask, panel_order, h, 2) for h in range(0, PANELS, 2)]
    work = (
        matrix.reshape(rows // tile, tile, nb_local, tile)
        * tile_mask.astype(jnp.float32)[:, None, :, None]
    ).reshape(rows, cols)
    both = [mine[h] + swap(mine[h], "col", pair) for h in range(2)]
    part = [lax.dynamic_slice_in_dim(x, core * tile, tile, 1) for x in both]
    for bit in others:
        part[0] = part[0] + swap(part[0], "col", bit)
    first = side_by_side(part[0], swap(part[0], "col", pair))

    last = len(order) - 1
    swapped = [order[1], order[0]] + order[2:]

    def halve(x, bit, *gates):
        keep, send = halves(x, has("row", bit))
        got = swap(send, "row", bit)
        return after(keep, *gates) + got

    def add(x, bit, *gates):
        got = swap(x, "row", bit)
        return after(x, *gates) + got

    def double(x, axis, bit, *gates):
        got = swap(x, axis, bit)
        return join(after(x, *gates), got, has(axis, bit))

    early = order[:last]
    crossed = swapped[:last]
    sent_a = []

    gram_a = share_of(dot_t(first, first))
    cross_a = dot_t(after(first, gram_a), work, MID)
    wait = [(cross_a,)] + [()] * last
    for k, bit in enumerate(order):
        sent_a.append(gram_a)
        gram_a = add(gram_a, bit, *wait[k])
    part[1] = after(part[1], part[0])
    for k, bit in enumerate(others):
        got = swap(part[1], "col", bit)
        part[1] = (part[1] if k else after(part[1], sent_a[last])) + got
    second = side_by_side(part[1], swap(part[1], "col", pair))
    for bit in others:
        gram_a = double(gram_a, "col", bit)
    gram_a_other = swap(gram_a, "col", pair)

    gram_b = jnp.concatenate([share_of(dot_t(second, first)), share_of(dot_t(second, second))], 1)
    cross_b = dot_t(after(second, gram_b), work, MID)
    cross_a = halve(cross_a, early[0], gram_b)
    f0, top0, rest, below = factor_step(0, tile, dtype, after(gram_a, cross_b), gram_a_other)
    gram_b = add(gram_b, order[0], f0)
    f1, top1 = factor_step(1, tile, dtype, after(rest, gram_b), below)
    for bit in early[1:]:
        cross_a = halve(cross_a, bit, f1)
    for k, bit in enumerate(order[1:]):
        gram_b = add(gram_b, bit, *((f1,) if k == 0 else ()))
        if k == 0:
            third = gram_b
    cross_b = halve(cross_b, crossed[0], third)
    for bit in crossed[1:]:
        cross_b = halve(cross_b, bit, gram_b)
    for bit in others:
        gram_b = double(gram_b, "col", bit)
    gram_b_other = swap(gram_b, "col", pair)
    f2, top2, rest, below = factor_step(2, tile, dtype, gram_b, gram_b_other, top0, top1)
    cross_a = add(cross_a, order[last], gram_b)
    cross_b = add(cross_b, order[last], f2)
    f3, inverse = factor_step(3, tile, dtype, rest, below, top0, top1, top2)
    for k, bit in enumerate(reversed(early)):
        cross_a = double(cross_a, "row", bit, f3 if k else f2)
    for bit in reversed(crossed):
        back_b = cross_b
        cross_b = double(cross_b, "row", bit, f3)
    width = 2 * tile
    basis = dot_nt(jnp.concatenate([after(first, back_b, f3), second], 1), inverse, MID)
    proj1 = jnp.dot(inverse[:width, :width], cross_a, precision=MID)
    work = lax.optimization_barrier(work - jnp.dot(basis[:, :width], proj1, precision=MID))
    proj2 = jnp.dot(inverse[width:, :width], cross_a, precision=MID) + jnp.dot(inverse[width:, width:], cross_b, precision=MID)
    work = work - jnp.dot(basis[:, width:], proj2, precision=MID)
    proj = jnp.concatenate([proj1, proj2], 0)
    return jnp.stack([f0, f1, f2, f3]), proj.reshape(PANELS, tile, cols), work


def solution(mesh):
    return jax.shard_map(
        on_device,
        mesh=mesh,
        in_specs=(P("row", "col"), P("row", "col"), P()),
        out_specs=(P(), P(None, None, "col"), P("row", "col")),
        check_vma=False,
    )
```

profile of v0, /device:TPU:0, one launch (start us, length us, event | category | flops | bytes accessed | tf_op | source)
XLA Modules:
  0.0 150.6 jit_solution(1220051543556089112)
XLA Ops:
  0.6 2.9 %shard_map.58 = f32[1024,256]{1,0:T(8,128)} custom-call(s32[32]{0:T(128)} %refs_0_.3, s32[8,8]{1,0:T(8,128)} %refs_1_.3, f32[1024,1024]{1,0:T(8,128)} %refs_2_.3), custom_call_target="tpu_custom_call" | custom-call | tf_op jit(solution)/shard_map/pallas_call | solution.py:67
  4.0 2.9 %shard_map.59 = f32[1024,256]{1,0:T(8,128)} custom-call(s32[32]{0:T(128)} %refs_0_.3, s32[8,8]{1,0:T(8,128)} %refs_1_.3, f32[1024,1024]{1,0:T(8,128)} %refs_2_.3), custom_call_target="tpu_custom_call" | custom-call | tf_op jit(solution)/shard_map/pallas_call | solution.py:67
  7.1 2.9 %collective-permute-start.1 = (f32[1024,128]{1,0:T(8,128)S(1)}, f32[1024,128]{1,0:T(8,128)S(1)}, u32[]{:S(2)}, u32[]{:S(2)}) collective-permute-start(f32[1024,128]{1,0:T(8,128)S(1)} %dynamic-slice_add_fusion.1), channel_id=1, source_target_pairs={{0,2},{1,3},{2,0},{3,1},{4,6},{5,7},{6,4},{7,5},{8,10},{9,11},{10,... | collective-permute-start | bytes 1572872 | tf_op jit(solution)/shard_map/ppermute | solution.py:16
  10.0 12.2 %collective-permute-done.1 = f32[1024,128]{1,0:T(8,128)S(1)} collective-permute-done((f32[1024,128]{1,0:T(8,128)S(1)}, f32[1024,128]{1,0:T(8,128)S(1)}, u32[]{:S(2)}, u32[]{:S(2)}) %collective-permute-start.1) | collective-permute-done | bytes 524320 | tf_op jit(solution)/shard_map/ppermute | solution.py:16
  22.5 1.1 dynamic-slice_add_fusion
  23.6 1.8 %collective-permute-start.8 = (f32[1024,128]{1,0:T(8,128)S(1)}, f32[1024,128]{1,0:T(8,128)S(1)}, u32[]{:S(2)}, u32[]{:S(2)}) collective-permute-start(f32[1024,128]{1,0:T(8,128)S(1)} %dynamic-slice_add_fusion), channel_id=1, source_target_pairs={{0,2},{1,3},{2,0},{3,1},{4,6},{5,7},{6,4},{7,5},{8,10},{9,11},{10,... | collective-permute-start | bytes 1572872 | tf_op jit(solution)/shard_map/ppermute | solution.py:16
  25.5 1.8 %fusion.25 = f32[256,256]{1,0:T(8,128)S(1)} fusion(f32[1024,256]{1,0:T(8,128)S(1)} %maximum_select_fusion), kind=kOutput, calls=%fused_computation.53 | convolution fusion | flops 805306368 | bytes 1310720 | tf_op jit(solution)/shard_map/dot_general | solution.py:41
  27.3 1.6 %collective-permute-start.3 = (f32[64,256]{1,0:T(8,128)S(1)}, f32[64,256]{1,0:T(8,128)S(1)}, u32[]{:S(2)}, u32[]{:S(2)}) collective-permute-start(f32[64,256]{1,0:T(8,128)S(1)} %constant_dynamic-slice_fusion.10), channel_id=1, source_target_pairs={{0,4},{4,0},{8,12},{12,8},{16,20},{20,16},{24,28},{28,24},{1,5},{5... | collective-permute-start | bytes 196616 | tf_op jit(solution)/shard_map/ppermute | solution.py:16
  29.2 2.8 %fusion.24 = f32[256,1024]{1,0:T(8,128)S(1)} fusion(f32[1024,256]{1,0:T(8,128)S(1)} %maximum_select_fusion, f32[1024,1024]{1,0:T(8,128)S(1)} %copy-done, f32[128,8,8,128]{3,2,1,0:T(8,128)S(1)} %bitcast.24), kind=kOutput, calls=%fused_computation.52 | convolution fusion | flops 1611661312 | bytes 10485760 | tf_op jit(solution)/shard_map/dot_general | solution.py:41
  32.1 1.6 %collective-permute-start.4 = (f32[64,256]{1,0:T(8,128)S(1)}, f32[64,256]{1,0:T(8,128)S(1)}, u32[]{:S(2)}, u32[]{:S(2)}) collective-permute-start(f32[64,256]{1,0:T(8,128)S(1)} %add.118), channel_id=1, source_target_pairs={{0,8},{4,12},{8,0},{12,4},{16,24},{20,28},{24,16},{28,20},{1,9},{5... | collective-permute-start | bytes 196616 | tf_op jit(solution)/shard_map/ppermute | solution.py:16
  33.7 2.7 %collective-permute-done.4 = f32[64,256]{1,0:T(8,128)S(1)} collective-permute-done((f32[64,256]{1,0:T(8,128)S(1)}, f32[64,256]{1,0:T(8,128)S(1)}, u32[]{:S(2)}, u32[]{:S(2)}) %collective-permute-start.4) | collective-permute-done | bytes 65568 | tf_op jit(solution)/shard_map/ppermute | solution.py:16
  36.4 1.5 %collective-permute-done.8 = f32[1024,128]{1,0:T(8,128)S(1)} collective-permute-done((f32[1024,128]{1,0:T(8,128)S(1)}, f32[1024,128]{1,0:T(8,128)S(1)}, u32[]{:S(2)}, u32[]{:S(2)}) %collective-permute-start.8) | collective-permute-done | bytes 524320 | tf_op jit(solution)/shard_map/ppermute | solution.py:16
  38.1 2.9 %collective-permute-start.5 = (f32[64,256]{1,0:T(8,128)S(1)}, f32[64,256]{1,0:T(8,128)S(1)}, u32[]{:S(2)}, u32[]{:S(2)}) collective-permute-start(f32[64,256]{1,0:T(8,128)S(1)} %add.119), channel_id=1, source_target_pairs={{0,16},{4,20},{8,24},{12,28},{16,0},{20,4},{24,8},{28,12},{1,17},{... | collective-permute-start | bytes 196616 | tf_op jit(solution)/shard_map/ppermute | solution.py:16
  41.0 0.9 constant_dynamic-slice_fusion.6
  41.9 1.5 collective-permute-start.16
  43.4 1.6 %collective-permute-done.5 = f32[64,256]{1,0:T(8,128)S(1)} collective-permute-done((f32[64,256]{1,0:T(8,128)S(1)}, f32[64,256]{1,0:T(8,128)S(1)}, u32[]{:S(2)}, u32[]{:S(2)}) %collective-permute-start.5) | collective-permute-done | bytes 65568 | tf_op jit(solution)/shard_map/ppermute | solution.py:16
  45.1 1.6 %collective-permute-start.6 = (f32[64,256]{1,0:T(8,128)S(1)}, f32[64,256]{1,0:T(8,128)S(1)}, u32[]{:S(2)}, u32[]{:S(2)}) collective-permute-start(f32[64,256]{1,0:T(8,128)S(1)} %add.120), channel_id=1, source_target_pairs={{0,2},{1,3},{2,0},{3,1},{4,6},{5,7},{6,4},{7,5},{8,10},{9,11},{10,... | collective-permute-start | bytes 196616 | tf_op jit(solution)/shard_map/ppermute | solution.py:16
  46.7 1.4 maximum_select_fusion.1
  48.1 1.8 %fusion.27 = f32[256,256]{1,0:T(8,128)S(1)} fusion(f32[1024,256]{1,0:T(8,128)S(1)} %maximum_select_fusion.1), kind=kOutput, calls=%fused_computation.55 | convolution fusion | flops 805306368 | bytes 1310720 | tf_op jit(solution)/shard_map/dot_general | solution.py:41
  49.9 1.8 %fusion.26 = f32[256,256]{1,0:T(8,128)S(1)} fusion(f32[1024,256]{1,0:T(8,128)S(1)} %maximum_select_fusion.1, f32[1024,256]{1,0:T(8,128)S(1)} %maximum_select_fusion), kind=kOutput, calls=%fused_computation.54 | convolution fusion | flops 805306368 | bytes 2359296 | tf_op jit(solution)/shard_map/dot_general | solution.py:41
  51.8 3.0 %fusion.23 = f32[256,1024]{1,0:T(8,128)S(1)} fusion(f32[1024,256]{1,0:T(8,128)S(1)} %maximum_select_fusion.1, f32[1024,1024]{1,0:T(8,128)S(1)} %copy-done.1, f32[128,8,8,128]{3,2,1,0:T(8,128)S(1)} %bitcast.25), kind=kOutput, calls=%fused_computation.51 | convolution fusion | flops 1611661312 | bytes 10485760 | tf_op jit(solution)/shard_map/dot_general | solution.py:41
  54.8 0.9 constant_dynamic-slice_fusion.2
  56.5 1.6 %collective-permute-start.11 = (f32[64,512]{1,0:T(8,128)S(1)}, f32[64,512]{1,0:T(8,128)S(1)}, u32[]{:S(2)}, u32[]{:S(2)}) collective-permute-start(f32[64,512]{1,0:T(8,128)S(1)} %pad_maximum_fusion.2), channel_id=1, source_target_pairs={{0,4},{4,0},{8,12},{12,8},{16,20},{20,16},{24,28},{28,24},{1,5},{5... | collective-permute-start | bytes 393224 | tf_op jit(solution)/shard_map/ppermute | solution.py:16
  58.1 7.4 %shard_map.60 = (f32[128,128]{1,0:T(8,128)}, f32[128,128]{1,0:T(8,128)}, f32[128,128]{1,0:T(8,128)}, f32[128,128]{1,0:T(8,128)}) custom-call(f32[128,256]{1,0:T(8,128)} %copy-done.9, f32[128,256]{1,0:T(8,128)} %collective-permute-done.10.refs_1_), custom_call_target="tpu_custom_call" | custom-call | tf_op jit(solution)/shard_map/pallas_call | solution.py:203
  65.5 1.1 add.130
  66.6 1.4 collective-permute-start.12
  68.8 7.0 %shard_map.61 = (f32[128,128]{1,0:T(8,128)}, f32[128,256]{1,0:T(8,128)}) custom-call(f32[128,128]{1,0:T(8,128)} %get-tuple-element.44.refs_0_, f32[128,128]{1,0:T(8,128)} %get-tuple-element.45.refs_1_), custom_call_target="tpu_custom_call" | custom-call | tf_op jit(solution)/shard_map/pallas_call | solution.py:203
  75.8 0.9 add.124
  76.7 3.4 %collective-permute-start.13 = (f32[64,512]{1,0:T(8,128)S(1)}, f32[64,512]{1,0:T(8,128)S(1)}, u32[]{:S(2)}, u32[]{:S(2)}) collective-permute-start(f32[64,512]{1,0:T(8,128)S(1)} %add.124), channel_id=1, source_target_pairs={{0,16},{4,20},{8,24},{12,28},{16,0},{20,4},{24,8},{28,12},{1,17},{... | collective-permute-start | bytes 393224 | tf_op jit(solution)/shard_map/ppermute | solution.py:16
  80.1 1.1 add.137
  81.3 1.5 collective-permute-start.22
  82.7 3.4 %collective-permute-done.13 = f32[64,512]{1,0:T(8,128)S(1)} collective-permute-done((f32[64,512]{1,0:T(8,128)S(1)}, f32[64,512]{1,0:T(8,128)S(1)}, u32[]{:S(2)}, u32[]{:S(2)}) %collective-permute-start.13) | collective-permute-done | bytes 131104 | tf_op jit(solution)/shard_map/ppermute | solution.py:16
  86.9 4.7 %collective-permute-done.14 = f32[64,512]{1,0:T(8,128)S(1)} collective-permute-done((f32[64,512]{1,0:T(8,128)S(1)}, f32[64,512]{1,0:T(8,128)S(1)}, u32[]{:S(2)}, u32[]{:S(2)}) %collective-permute-start.14) | collective-permute-done | bytes 131104 | tf_op jit(solution)/shard_map/ppermute | solution.py:16
  91.9 13.9 %collective-permute-done.18 = f32[64,1024]{1,0:T(8,128)S(1)} collective-permute-done((f32[64,1024]{1,0:T(8,128)S(1)}, f32[64,1024]{1,0:T(8,128)S(1)}, u32[]{:S(2)}, u32[]{:S(2)}) %collective-permute-start.18) | collective-permute-done | bytes 262176 | tf_op jit(solution)/shard_map/ppermute | solution.py:16
  106.6 9.0 %shard_map.62 = (f32[128,128]{1,0:T(8,128)}, f32[128,384]{1,0:T(8,128)}, f32[128,128]{1,0:T(8,128)}, f32[128,384]{1,0:T(8,128)}) custom-call(f32[128,512]{1,0:T(8,128)} %copy-done.8, f32[128,512]{1,0:T(8,128)} %copy-done.10, f32[128,128]{1,0:T(8,128)} %get-tuple-element.48.refs_2_, f32[128,256]{1,0:T(8,128)} %get-tuple-element.49.refs_3_), custom_call_target="tpu_custom_call" | custom-call | tf_op jit(solution)/shard_map/pallas_call | solution.py:203
  115.7 1.5 collective-permute-start.24
  117.1 1.1 maximum_select_fusion.7
  118.2 1.4 collective-permute-start.20
  119.6 7.9 %shard_map.63 = (f32[128,128]{1,0:T(8,128)}, f32[512,512]{1,0:T(8,128)}) custom-call(f32[128,128]{1,0:T(8,128)} %get-tuple-element.51.refs_0_, f32[128,384]{1,0:T(8,128)} %get-tuple-element.52.refs_1_, f32[128,128]{1,0:T(8,128)} %get-tuple-element.48.refs_2_, f32[128,256]{1,0:T(8,128)} %get-tuple-element.49.refs_3_, f32[128,384]{1,0:T(8,128)} %get-tuple-element.53.refs_4_), custom_call_target="tpu_custom_call" | custom-call | tf_op jit(solution)/shard_map/pallas_call | solution.py:203
  127.5 1.7 %pad_maximum_fusion.1 = f32[4,128,128]{2,1,0:T(8,128)} fusion(f32[1,128,128]{2,1,0:T(8,128)} %bitcast.31, f32[1,128,128]{2,1,0:T(8,128)} %bitcast.30, f32[1,128,128]{2,1,0:T(8,128)} %bitcast.29, f32[1,128,128]{2,1,0:T(8,128)} %bitcast.28), kind=kLoop, calls=%fused_computation.30 | loop fusion | flops 196608 | bytes 524288 | tf_op jit(solution)/shard_map/stack | solution.py:306
  129.1 1.2 maximum_select_fusion.8
  130.4 1.4 collective-permute-start.25
  131.7 3.1 %fusion = f32[1024,512]{1,0:T(8,128)S(1)} fusion(f32[512,512]{1,0:T(8,128)} %get-tuple-element.55, f32[1024,256]{1,0:T(8,128)S(1)} %maximum_select_fusion.1, f32[1024,256]{1,0:T(8,128)S(1)} %maximum_select_fusion), kind=kOutput, calls=%fused_computation.4 | convolution fusion | flops 1611137024 | bytes 5242880 | tf_op jit(solution)/shard_map/dot_general | solution.py:45
  135.1 1.6 %fusion.12 = f32[256,1024]{1,0:T(8,128)S(1)} fusion(f32[128,1024]{1,0:T(8,128)S(1)} %collective-permute-done.20, f32[128,1024]{1,0:T(8,128)S(1)} %maximum_select_fusion.7, pred[]{:T(512)S(6)} %eq.30, f32[512,512]{1,0:T(8,128)} %get-tuple-element.55), kind=kOutput, calls=%fused_computation.21 | convolution fusion | flops 403439616 | bytes 2359297 | tf_op jit(solution)/shard_map/dot_general | solution.py:301
  136.7 2.5 %convolution_subtract_fusion.1 = f32[1024,1024]{1,0:T(8,128)S(1)} fusion(f32[256,1024]{1,0:T(8,128)S(1)} %fusion.12, f32[1024,512]{1,0:T(8,128)S(1)} %fusion, f32[1024,1024]{1,0:T(8,128)S(1)} %copy-done.2, f32[128,8,8,128]{3,2,1,0:T(8,128)S(1)} %bitcast.26), kind=kOutput, calls=%fused_computation.2 | convolution fusion | flops 1612709888 | bytes 14680064 | tf_op jit(solution)/shard_map/dot_general | solution.py:302
  139.2 4.8 %collective-permute-done.25 = f32[128,1024]{1,0:T(8,128)S(1)} collective-permute-done((f32[128,1024]{1,0:T(8,128)S(1)}, f32[128,1024]{1,0:T(8,128)S(1)}, u32[]{:S(2)}, u32[]{:S(2)}) %collective-permute-start.25) | collective-permute-done | bytes 524320 | tf_op jit(solution)/shard_map/ppermute | solution.py:16
  145.3 1.5 pad_maximum_fusion
  146.8 3.8 %convolution_subtract_fusion = f32[1024,1024]{1,0:T(8,128)} fusion(f32[1024,1024]{1,0:T(8,128)S(1)} %convolution_subtract_fusion.1, f32[256,1024]{1,0:T(8,128)S(1)} %convolution_add_fusion, f32[1024,512]{1,0:T(8,128)S(1)} %fusion), kind=kOutput, calls=%fused_computation.1 | convolution fusion | flops 1611661312 | bytes 10485760 | tf_op jit(solution)/shard_map/dot_general | solution.py:304
  (78 shorter events, 6.5 us)
Async XLA Ops:
  3.5 3.5 %copy-start.7 = (f32[1024,256]{1,0:T(8,128)S(1)}, f32[1024,256]{1,0:T(8,128)}, u32[]{:S(2)}) copy-start(f32[1024,256]{1,0:T(8,128)} %shard_map.58) | copy-start | bytes 3145732
  3.5 18.9 %copy-start.11 = (s32[8,8]{1,0:T(8,128)S(1)}, s32[8,8]{1,0:T(8,128)}, u32[]{:S(2)}) copy-start(s32[8,8]{1,0:T(8,128)} %refs_1_.3) | copy-start | bytes 772
  3.5 3.5 %collective-permute-start = (f32[1024,256]{1,0:T(8,128)}, f32[1024,256]{1,0:T(8,128)S(1)}, u32[]{:S(2)}, u32[]{:S(2)}) collective-permute-start(f32[1024,256]{1,0:T(8,128)} %shard_map.58), channel_id=1, source_target_pairs={{0,1},{1,0},{2,3},{3,2},{4,5},{5,4},{6,7},{7,6},{8,9},{9,8},{10,11... | collective-permute-start | bytes 3145736 | tf_op jit(solution)/shard_map/ppermute | solution.py:16
  6.9 15.6 %collective-permute-start.7 = (f32[1024,256]{1,0:T(8,128)}, f32[1024,256]{1,0:T(8,128)S(1)}, u32[]{:S(2)}, u32[]{:S(2)}) collective-permute-start(f32[1024,256]{1,0:T(8,128)} %shard_map.59), channel_id=1, source_target_pairs={{0,1},{1,0},{2,3},{3,2},{4,5},{5,4},{6,7},{7,6},{8,9},{9,8},{10,11... | collective-permute-start | bytes 3145736 | tf_op jit(solution)/shard_map/ppermute | solution.py:16
  7.1 15.2 %collective-permute-start.1 = (f32[1024,128]{1,0:T(8,128)S(1)}, f32[1024,128]{1,0:T(8,128)S(1)}, u32[]{:S(2)}, u32[]{:S(2)}) collective-permute-start(f32[1024,128]{1,0:T(8,128)S(1)} %dynamic-slice_add_fusion.1), channel_id=1, source_target_pairs={{0,2},{1,3},{2,0},{3,1},{4,6},{5,7},{6,4},{7,5},{8,10},{9,11},{10,... | collective-permute-start | bytes 1572872 | tf_op jit(solution)/shard_map/ppermute | solution.py:16
  22.3 3.1 %collective-permute-start.2 = (f32[1024,128]{1,0:T(8,128)S(1)}, f32[1024,128]{1,0:T(8,128)S(1)}, u32[]{:S(2)}, u32[]{:S(2)}) collective-permute-start(f32[1024,128]{1,0:T(8,128)S(1)} %add.115), channel_id=1, source_target_pairs={{0,1},{1,0},{2,3},{3,2},{4,5},{5,4},{6,7},{7,6},{8,9},{9,8},{10,11... | collective-permute-start | bytes 1572872 | tf_op jit(solution)/shard_map/ppermute | solution.py:16
  23.6 5.7 %copy-start = (f32[1024,1024]{1,0:T(8,128)S(1)}, f32[1024,1024]{1,0:T(8,128)}, u32[]{:S(2)}) copy-start(f32[1024,1024]{1,0:T(8,128)} %refs_2_.3) | copy-start | bytes 12582916
  23.6 14.4 %collective-permute-start.8 = (f32[1024,128]{1,0:T(8,128)S(1)}, f32[1024,128]{1,0:T(8,128)S(1)}, u32[]{:S(2)}, u32[]{:S(2)}) collective-permute-start(f32[1024,128]{1,0:T(8,128)S(1)} %dynamic-slice_add_fusion), channel_id=1, source_target_pairs={{0,2},{1,3},{2,0},{3,1},{4,6},{5,7},{6,4},{7,5},{8,10},{9,11},{10,... | collective-permute-start | bytes 1572872 | tf_op jit(solution)/shard_map/ppermute | solution.py:16
  27.3 4.7 %collective-permute-start.3 = (f32[64,256]{1,0:T(8,128)S(1)}, f32[64,256]{1,0:T(8,128)S(1)}, u32[]{:S(2)}, u32[]{:S(2)}) collective-permute-start(f32[64,256]{1,0:T(8,128)S(1)} %constant_dynamic-slice_fusion.10), channel_id=1, source_target_pairs={{0,4},{4,0},{8,12},{12,8},{16,20},{20,16},{24,28},{28,24},{1,5},{5... | collective-permute-start | bytes 196616 | tf_op jit(solution)/shard_map/ppermute | solution.py:16
  29.2 2.8 %copy-start.3 = (f32[8,128,8,128]{3,2,1,0:T(8,128)}, f32[8,128,8,128]{3,2,1,0:T(8,128)S(1)}, u32[]{:S(2)}) copy-start(f32[8,128,8,128]{3,2,1,0:T(8,128)S(1)} %mul.50) | copy-start | bytes 12582916
  32.1 4.3 %collective-permute-start.4 = (f32[64,256]{1,0:T(8,128)S(1)}, f32[64,256]{1,0:T(8,128)S(1)}, u32[]{:S(2)}, u32[]{:S(2)}) collective-permute-start(f32[64,256]{1,0:T(8,128)S(1)} %add.118), channel_id=1, source_target_pairs={{0,8},{4,12},{8,0},{12,4},{16,24},{20,28},{24,16},{28,20},{1,9},{5... | collective-permute-start | bytes 196616 | tf_op jit(solution)/shard_map/ppermute | solution.py:16
  38.0 8.7 %collective-permute-start.9 = (f32[1024,128]{1,0:T(8,128)S(1)}, f32[1024,128]{1,0:T(8,128)}, u32[]{:S(2)}, u32[]{:S(2)}) collective-permute-start(f32[1024,128]{1,0:T(8,128)S(1)} %add.122), channel_id=1, source_target_pairs={{0,1},{1,0},{2,3},{3,2},{4,5},{5,4},{6,7},{7,6},{8,9},{9,8},{10,11... | collective-permute-start | bytes 1572872 | tf_op jit(solution)/shard_map/ppermute | solution.py:16
  38.1 6.9 %collective-permute-start.5 = (f32[64,256]{1,0:T(8,128)S(1)}, f32[64,256]{1,0:T(8,128)S(1)}, u32[]{:S(2)}, u32[]{:S(2)}) collective-permute-start(f32[64,256]{1,0:T(8,128)S(1)} %add.119), channel_id=1, source_target_pairs={{0,16},{4,20},{8,24},{12,28},{16,0},{20,4},{24,8},{28,12},{1,17},{... | collective-permute-start | bytes 196616 | tf_op jit(solution)/shard_map/ppermute | solution.py:16
  41.0 10.8 %copy-start.4 = (f32[8,128,8,128]{3,2,1,0:T(8,128)S(1)}, f32[8,128,8,128]{3,2,1,0:T(8,128)}, u32[]{:S(2)}) copy-start(f32[8,128,8,128]{3,2,1,0:T(8,128)} %copy-done.3) | copy-start | bytes 12582916
  41.9 9.9 %copy-start.1 = (f32[1024,1024]{1,0:T(8,128)S(1)}, f32[1024,1024]{1,0:T(8,128)}, u32[]{:S(2)}) copy-start(f32[1024,1024]{1,0:T(8,128)} %refs_2_.3) | copy-start | bytes 12582916
  41.9 23.5 %collective-permute-start.16 = (f32[128,1024]{1,0:T(8,128)}, f32[128,1024]{1,0:T(8,128)}, u32[]{:S(2)}, u32[]{:S(2)}) collective-permute-start(f32[128,1024]{1,0:T(8,128)} %get-tuple-element.67), channel_id=1, source_target_pairs={{0,4},{4,0},{8,12},{12,8},{16,20},{20,16},{24,28},{28,24},{1,5},{5... | collective-permute-start | bytes 1572872 | tf_op jit(solution)/shard_map/ppermute | solution.py:16
  45.1 11.3 %collective-permute-start.6 = (f32[64,256]{1,0:T(8,128)S(1)}, f32[64,256]{1,0:T(8,128)S(1)}, u32[]{:S(2)}, u32[]{:S(2)}) collective-permute-start(f32[64,256]{1,0:T(8,128)S(1)} %add.120), channel_id=1, source_target_pairs={{0,2},{1,3},{2,0},{3,1},{4,6},{5,7},{6,4},{7,5},{8,10},{9,11},{10,... | collective-permute-start | bytes 196616 | tf_op jit(solution)/shard_map/ppermute | solution.py:16
  55.7 24.4 %collective-permute-start.21 = (f32[128,1024]{1,0:T(8,128)}, f32[128,1024]{1,0:T(8,128)}, u32[]{:S(2)}, u32[]{:S(2)}) collective-permute-start(f32[128,1024]{1,0:T(8,128)} %get-tuple-element.69), channel_id=1, source_target_pairs={{0,8},{4,12},{8,0},{12,4},{16,24},{20,28},{24,16},{28,20},{1,9},{5... | collective-permute-start | bytes 1572872 | tf_op jit(solution)/shard_map/ppermute | solution.py:16
  56.4 1.7 %copy-start.9 = (f32[128,256]{1,0:T(8,128)}, f32[128,256]{1,0:T(8,128)S(1)}, u32[]{:S(2)}) copy-start(f32[128,256]{1,0:T(8,128)S(1)} %maximum_select_fusion.10.refs_0_) | copy-start | bytes 393220
  56.4 1.6 %collective-permute-start.10 = (f32[128,256]{1,0:T(8,128)S(1)}, f32[128,256]{1,0:T(8,128)}, u32[]{:S(2)}, u32[]{:S(2)}) collective-permute-start(f32[128,256]{1,0:T(8,128)S(1)} %maximum_select_fusion.10.refs_0_), channel_id=1, source_target_pairs={{0,1},{1,0},{2,3},{3,2},{4,5},{5,4},{6,7},{7,6},{8,9},{9,8},{10,11... | collective-permute-start | bytes 393224 | tf_op jit(solution)/shard_map/ppermute | solution.py:16
  56.5 10.1 %collective-permute-start.11 = (f32[64,512]{1,0:T(8,128)S(1)}, f32[64,512]{1,0:T(8,128)S(1)}, u32[]{:S(2)}, u32[]{:S(2)}) collective-permute-start(f32[64,512]{1,0:T(8,128)S(1)} %pad_maximum_fusion.2), channel_id=1, source_target_pairs={{0,4},{4,0},{8,12},{12,8},{16,20},{20,16},{24,28},{28,24},{1,5},{5... | collective-permute-start | bytes 393224 | tf_op jit(solution)/shard_map/ppermute | solution.py:16
  66.6 9.2 %collective-permute-start.12 = (f32[64,512]{1,0:T(8,128)S(1)}, f32[64,512]{1,0:T(8,128)}, u32[]{:S(2)}, u32[]{:S(2)}) collective-permute-start(f32[64,512]{1,0:T(8,128)S(1)} %add.123), channel_id=1, source_target_pairs={{0,8},{4,12},{8,0},{12,4},{16,24},{20,28},{24,16},{28,20},{1,9},{5... | collective-permute-start | bytes 393224 | tf_op jit(solution)/shard_map/ppermute | solution.py:16
  68.0 18.8 %collective-permute-start.17 = (f32[64,1024]{1,0:T(8,128)S(1)}, f32[64,1024]{1,0:T(8,128)S(1)}, u32[]{:S(2)}, u32[]{:S(2)}) collective-permute-start(f32[64,1024]{1,0:T(8,128)S(1)} %get-tuple-element.71), channel_id=1, source_target_pairs={{0,8},{4,12},{8,0},{12,4},{16,24},{20,28},{24,16},{28,20},{1,9},{5... | collective-permute-start | bytes 786440 | tf_op jit(solution)/shard_map/ppermute | solution.py:16
  76.7 9.5 %collective-permute-start.13 = (f32[64,512]{1,0:T(8,128)S(1)}, f32[64,512]{1,0:T(8,128)S(1)}, u32[]{:S(2)}, u32[]{:S(2)}) collective-permute-start(f32[64,512]{1,0:T(8,128)S(1)} %add.124), channel_id=1, source_target_pairs={{0,16},{4,20},{8,24},{12,28},{16,0},{20,4},{24,8},{28,12},{1,17},{... | collective-permute-start | bytes 393224 | tf_op jit(solution)/shard_map/ppermute | solution.py:16
  81.3 10.5 %collective-permute-start.22 = (f32[64,1024]{1,0:T(8,128)S(1)}, f32[64,1024]{1,0:T(8,128)S(1)}, u32[]{:S(2)}, u32[]{:S(2)}) collective-permute-start(f32[64,1024]{1,0:T(8,128)S(1)} %get-tuple-element.73), channel_id=1, source_target_pairs={{0,4},{4,0},{8,12},{12,8},{16,20},{20,16},{24,28},{28,24},{1,5},{5... | collective-permute-start | bytes 786440 | tf_op jit(solution)/shard_map/ppermute | solution.py:16
  86.2 5.4 %collective-permute-start.14 = (f32[64,512]{1,0:T(8,128)S(1)}, f32[64,512]{1,0:T(8,128)S(1)}, u32[]{:S(2)}, u32[]{:S(2)}) collective-permute-start(f32[64,512]{1,0:T(8,128)S(1)} %add.125), channel_id=1, source_target_pairs={{0,2},{1,3},{2,0},{3,1},{4,6},{5,7},{6,4},{7,5},{8,10},{9,11},{10,... | collective-permute-start | bytes 393224 | tf_op jit(solution)/shard_map/ppermute | solution.py:16
  86.8 19.0 %collective-permute-start.18 = (f32[64,1024]{1,0:T(8,128)S(1)}, f32[64,1024]{1,0:T(8,128)S(1)}, u32[]{:S(2)}, u32[]{:S(2)}) collective-permute-start(f32[64,1024]{1,0:T(8,128)S(1)} %add.133), channel_id=1, source_target_pairs={{0,16},{4,20},{8,24},{12,28},{16,0},{20,4},{24,8},{28,12},{1,17},{... | collective-permute-start | bytes 786440 | tf_op jit(solution)/shard_map/ppermute | solution.py:16
  91.6 15.0 %copy-start.8 = (f32[128,512]{1,0:T(8,128)}, f32[128,512]{1,0:T(8,128)S(1)}, u32[]{:S(2)}) copy-start(f32[128,512]{1,0:T(8,128)S(1)} %maximum_select_fusion.9.refs_0_) | copy-start | bytes 786436
  91.7 14.3 %collective-permute-start.15 = (f32[128,512]{1,0:T(8,128)S(1)}, f32[128,512]{1,0:T(8,128)S(1)}, u32[]{:S(2)}, u32[]{:S(2)}) collective-permute-start(f32[128,512]{1,0:T(8,128)S(1)} %maximum_select_fusion.9.refs_0_), channel_id=1, source_target_pairs={{0,1},{1,0},{2,3},{3,2},{4,5},{5,4},{6,7},{7,6},{8,9},{9,8},{10,11... | collective-permute-start | bytes 786440 | tf_op jit(solution)/shard_map/ppermute | solution.py:16
  91.8 23.8 %collective-permute-start.23 = (f32[64,1024]{1,0:T(8,128)S(1)}, f32[64,1024]{1,0:T(8,128)S(1)}, u32[]{:S(2)}, u32[]{:S(2)}) collective-permute-start(f32[64,1024]{1,0:T(8,128)S(1)} %add.140), channel_id=1, source_target_pairs={{0,16},{4,20},{8,24},{12,28},{16,0},{20,4},{24,8},{28,12},{1,17},{... | collective-permute-start | bytes 786440 | tf_op jit(solution)/shard_map/ppermute | solution.py:16
  105.8 11.3 %collective-permute-start.19 = (f32[64,1024]{1,0:T(8,128)S(1)}, f32[64,1024]{1,0:T(8,128)}, u32[]{:S(2)}, u32[]{:S(2)}) collective-permute-start(f32[64,1024]{1,0:T(8,128)S(1)} %add.134), channel_id=1, source_target_pairs={{0,8},{4,12},{8,0},{12,4},{16,24},{20,28},{24,16},{28,20},{1,9},{5... | collective-permute-start | bytes 786440 | tf_op jit(solution)/shard_map/ppermute | solution.py:16
  105.9 0.7 copy-start.10
  115.7 13.5 %collective-permute-start.24 = (f32[64,1024]{1,0:T(8,128)S(1)}, f32[64,1024]{1,0:T(8,128)}, u32[]{:S(2)}, u32[]{:S(2)}) collective-permute-start(f32[64,1024]{1,0:T(8,128)S(1)} %add.141), channel_id=1, source_target_pairs={{0,4},{4,0},{8,12},{12,8},{16,20},{20,16},{24,28},{28,24},{1,5},{5... | collective-permute-start | bytes 786440 | tf_op jit(solution)/shard_map/ppermute | solution.py:16
  118.2 16.9 %collective-permute-start.20 = (f32[128,1024]{1,0:T(8,128)S(1)}, f32[128,1024]{1,0:T(8,128)S(1)}, u32[]{:S(2)}, u32[]{:S(2)}) collective-permute-start(f32[128,1024]{1,0:T(8,128)S(1)} %maximum_select_fusion.7), channel_id=1, source_target_pairs={{0,4},{4,0},{8,12},{12,8},{16,20},{20,16},{24,28},{28,24},{1,5},{5... | collective-permute-start | bytes 1572872 | tf_op jit(solution)/shard_map/ppermute | solution.py:16
  129.1 7.6 %copy-start.2 = (f32[1024,1024]{1,0:T(8,128)S(1)}, f32[1024,1024]{1,0:T(8,128)}, u32[]{:S(2)}) copy-start(f32[1024,1024]{1,0:T(8,128)} %refs_2_.3) | copy-start | bytes 12582916
  129.1 7.6 %copy-start.5 = (f32[8,128,8,128]{3,2,1,0:T(8,128)S(1)}, f32[8,128,8,128]{3,2,1,0:T(8,128)}, u32[]{:S(2)}) copy-start(f32[8,128,8,128]{3,2,1,0:T(8,128)} %copy-done.3) | copy-start | bytes 12582916
  130.4 13.6 %collective-permute-start.25 = (f32[128,1024]{1,0:T(8,128)S(1)}, f32[128,1024]{1,0:T(8,128)S(1)}, u32[]{:S(2)}, u32[]{:S(2)}) collective-permute-start(f32[128,1024]{1,0:T(8,128)S(1)} %maximum_select_fusion.8), channel_id=1, source_target_pairs={{0,8},{4,12},{8,0},{12,4},{16,24},{20,28},{24,16},{28,20},{1,9},{5... | collective-permute-start | bytes 1572872 | tf_op jit(solution)/shard_map/ppermute | solution.py:16
  136.7 7.3 %copy-start.6 = (f32[512,512]{1,0:T(8,128)S(1)}, f32[512,512]{1,0:T(8,128)}, u32[]{:S(2)}) copy-start(f32[512,512]{1,0:T(8,128)} %get-tuple-element.55) | copy-start | bytes 3145732
where the time goes:
time: 151 us
  waiting for transfers between devices  45.3 us (30%)
  Pallas kernels  37 us (25%)
  starting transfers between devices  29.2 us (19%)
  matrix products  23.5 us (16%)
  other arithmetic  11.5 us (8%)
  local copies, waits for them, and re-layouts  3.03 us (2%)
    ppermute x26, waiting for transfers between devices, swap(): return lax.ppermute(x, axis, [(i, i ^ bit) for i in range(size)])  45.3 us
    pallas_call x4, Pallas kernels, factor_step(): pl.pallas_call(lambda *refs: factor_kernel(*refs, panel=panel, tile=tile)...  31.2 us
    ppermute x26, starting transfers between devices, swap(): return lax.ppermute(x, axis, [(i, i ^ bit) for i in range(size)])  29.2 us
    dot_general x5, matrix products, dot_t(): return lax.dot_general(a, b, (((0,), (0,)), ((), ())), precision=precision)  11.2 us
    pallas_call x2, Pallas kernels, cut_panels(): pl.pallas_call(lambda *refs: cut_kernel(*refs, first=first), grid_spec=pl...  5.74 us
    dot_general x1, matrix products, on_device(): work = work - jnp.dot(basis[:, width:], proj2, precision=MID)  3.85 us
    dot_general x1, matrix products, dot_nt(): return lax.dot_general(a, b, (((1,), (1,)), ((), ())), precision=precision)  3.05 us
  transfers between devices with their start and end apart: 26, of which 9 were waited for; matrix products, arithmetic and copies ran while one was open for 20% of the time, Pallas kernels for 23%

commit v1 on v0

--- a/solution.py
+++ b/solution.py
@@ -297,13 +297,16 @@
         back_b = cross_b
         cross_b = double(cross_b, "row", bit, f3)
     width = 2 * tile
-    basis = dot_nt(jnp.concatenate([after(first, back_b, f3), second], 1), inverse, MID)
+    basis1 = dot_nt(first, after(inverse[:width, :width], back_b), MID)
+    basis2 = dot_nt(first, after(inverse[width:, :width], back_b), MID) + dot_nt(second, inverse[width:, width:], MID)
+    factors = jnp.stack([f0, f1, f2, after(f3, back_b)])
     proj1 = jnp.dot(inverse[:width, :width], cross_a, precision=MID)
-    work = lax.optimization_barrier(work - jnp.dot(basis[:, :width], proj1, precision=MID))
+    proj = lax.optimization_barrier(jnp.pad(proj1, ((0, width), (0, 0))))
+    work = lax.optimization_barrier(work - jnp.dot(basis1, proj1, precision=MID))
     proj2 = jnp.dot(inverse[width:, :width], cross_a, precision=MID) + jnp.dot(inverse[width:, width:], cross_b, precision=MID)
-    work = work - jnp.dot(basis[:, width:], proj2, precision=MID)
-    proj = jnp.concatenate([proj1, proj2], 0)
-    return jnp.stack([f0, f1, f2, f3]), proj.reshape(PANELS, tile, cols), work
+    work = work - jnp.dot(basis2, proj2, precision=MID)
+    proj = lax.dynamic_update_slice(proj, proj2, (width, 0))
+    return factors, proj.reshape(PANELS, tile, cols), work
 
 
 def solution(mesh):

time: 151 us -> 153 us (1.013)
  waiting for transfers between devices: 45.3 us -> 49.7 us
  other arithmetic: 11.5 us -> 9.74 us
    ppermute x26, waiting for transfers between devices: 45.3 us -> 49.7 us  [swap(): return lax.ppermute(x, axis, [(i, i ^ bit) for i in range(size)])]
    add x4, other arithmetic: 2.27 us -> 4.16 us  [halve(): return after(keep, *gates) + got]
  transfers between devices with their start and end apart: 26 -> 26, of which waited for: 9 -> 9; matrix products, arithmetic and copies ran while one was open for 20% -> 19% of each run, Pallas kernels for 23% -> 22%
where the time goes in v1:
time: 153 us; the launch traced here: 152 us
  waiting for transfers between devices  49.7 us (32%)
  Pallas kernels  37 us (24%)
  starting transfers between devices  29.6 us (19%)
  matrix products  22.4 us (15%)
  other arithmetic  9.74 us (6%)
  local copies, waits for them, and re-layouts  2.58 us (2%)
    ppermute x26, waiting for transfers between devices, swap(): return lax.ppermute(x, axis, [(i, i ^ bit) for i in range(size)])  49.7 us
    pallas_call x4, Pallas kernels, factor_step(): pl.pallas_call(lambda *refs: factor_kernel(*refs, panel=panel, tile=tile)...  31.3 us
    ppermute x26, starting transfers between devices, swap(): return lax.ppermute(x, axis, [(i, i ^ bit) for i in range(size)])  29.6 us
    dot_general x5, matrix products, dot_t(): return lax.dot_general(a, b, (((0,), (0,)), ((), ())), precision=precision)  11.2 us
    pallas_call x2, Pallas kernels, cut_panels(): pl.pallas_call(lambda *refs: cut_kernel(*refs, first=first), grid_spec=pl...  5.74 us
    add x4, other arithmetic, halve(): return after(keep, *gates) + got  4.16 us
    dot_general x1, matrix products, on_device(): work = work - jnp.dot(basis2, proj2, precision=MID)  3.84 us
  transfers between devices with their start and end apart: 26, of which 9 were waited for; matrix products, arithmetic and copies ran while one was open for 19% of the time, Pallas kernels for 22%

profile of v1, /device:TPU:0, one launch (start us, length us, event | category | flops | bytes accessed | tf_op | source)
XLA Modules:
  0.0 152.3 jit_solution(2621198873624368126)
XLA Ops:
  0.6 2.9 %shard_map.58 = f32[1024,256]{1,0:T(8,128)} custom-call(s32[32]{0:T(128)} %refs_0_.3, s32[8,8]{1,0:T(8,128)} %refs_1_.3, f32[1024,1024]{1,0:T(8,128)} %refs_2_.3), custom_call_target="tpu_custom_call" | custom-call | tf_op jit(solution)/shard_map/pallas_call | solution.py:67
  4.0 2.9 %shard_map.59 = f32[1024,256]{1,0:T(8,128)} custom-call(s32[32]{0:T(128)} %refs_0_.3, s32[8,8]{1,0:T(8,128)} %refs_1_.3, f32[1024,1024]{1,0:T(8,128)} %refs_2_.3), custom_call_target="tpu_custom_call" | custom-call | tf_op jit(solution)/shard_map/pallas_call | solution.py:67
  7.1 2.9 %collective-permute-start.1 = (f32[1024,128]{1,0:T(8,128)S(1)}, f32[1024,128]{1,0:T(8,128)S(1)}, u32[]{:S(2)}, u32[]{:S(2)}) collective-permute-start(f32[1024,128]{1,0:T(8,128)S(1)} %dynamic-slice_add_fusion.1), channel_id=1, source_target_pairs={{0,2},{1,3},{2,0},{3,1},{4,6},{5,7},{6,4},{7,5},{8,10},{9,11},{10,... | collective-permute-start | bytes 1572872 | tf_op jit(solution)/shard_map/ppermute | solution.py:16
  10.0 12.2 %collective-permute-done.1 = f32[1024,128]{1,0:T(8,128)S(1)} collective-permute-done((f32[1024,128]{1,0:T(8,128)S(1)}, f32[1024,128]{1,0:T(8,128)S(1)}, u32[]{:S(2)}, u32[]{:S(2)}) %collective-permute-start.1) | collective-permute-done | bytes 524320 | tf_op jit(solution)/shard_map/ppermute | solution.py:16
  22.5 1.1 dynamic-slice_add_fusion
  23.6 1.8 %collective-permute-start.8 = (f32[1024,128]{1,0:T(8,128)S(1)}, f32[1024,128]{1,0:T(8,128)S(1)}, u32[]{:S(2)}, u32[]{:S(2)}) collective-permute-start(f32[1024,128]{1,0:T(8,128)S(1)} %dynamic-slice_add_fusion), channel_id=1, source_target_pairs={{0,2},{1,3},{2,0},{3,1},{4,6},{5,7},{6,4},{7,5},{8,10},{9,11},{10,... | collective-permute-start | bytes 1572872 | tf_op jit(solution)/shard_map/ppermute | solution.py:16
  25.5 1.8 %fusion.21 = f32[256,256]{1,0:T(8,128)S(1)} fusion(f32[1024,256]{1,0:T(8,128)S(1)} %maximum_select_fusion), kind=kOutput, calls=%fused_computation.50 | convolution fusion | flops 805306368 | bytes 1310720 | tf_op jit(solution)/shard_map/dot_general | solution.py:41
  27.3 1.6 %collective-permute-start.3 = (f32[64,256]{1,0:T(8,128)S(1)}, f32[64,256]{1,0:T(8,128)S(1)}, u32[]{:S(2)}, u32[]{:S(2)}) collective-permute-start(f32[64,256]{1,0:T(8,128)S(1)} %constant_dynamic-slice_fusion.10), channel_id=1, source_target_pairs={{0,4},{4,0},{8,12},{12,8},{16,20},{20,16},{24,28},{28,24},{1,5},{5... | collective-permute-start | bytes 196616 | tf_op jit(solution)/shard_map/ppermute | solution.py:16
  29.2 2.8 %fusion.19 = f32[256,1024]{1,0:T(8,128)S(1)} fusion(f32[1024,256]{1,0:T(8,128)S(1)} %maximum_select_fusion, f32[1024,1024]{1,0:T(8,128)S(1)} %copy-done, f32[128,8,8,128]{3,2,1,0:T(8,128)S(1)} %bitcast.30), kind=kOutput, calls=%fused_computation.48 | convolution fusion | flops 1611661312 | bytes 10485760 | tf_op jit(solution)/shard_map/dot_general | solution.py:41
  32.1 1.6 %collective-permute-start.4 = (f32[64,256]{1,0:T(8,128)S(1)}, f32[64,256]{1,0:T(8,128)S(1)}, u32[]{:S(2)}, u32[]{:S(2)}) collective-permute-start(f32[64,256]{1,0:T(8,128)S(1)} %add.123), channel_id=1, source_target_pairs={{0,8},{4,12},{8,0},{12,4},{16,24},{20,28},{24,16},{28,20},{1,9},{5... | collective-permute-start | bytes 196616 | tf_op jit(solution)/shard_map/ppermute | solution.py:16
  33.7 2.7 %collective-permute-done.4 = f32[64,256]{1,0:T(8,128)S(1)} collective-permute-done((f32[64,256]{1,0:T(8,128)S(1)}, f32[64,256]{1,0:T(8,128)S(1)}, u32[]{:S(2)}, u32[]{:S(2)}) %collective-permute-start.4) | collective-permute-done | bytes 65568 | tf_op jit(solution)/shard_map/ppermute | solution.py:16
  36.4 1.5 %collective-permute-done.8 = f32[1024,128]{1,0:T(8,128)S(1)} collective-permute-done((f32[1024,128]{1,0:T(8,128)S(1)}, f32[1024,128]{1,0:T(8,128)S(1)}, u32[]{:S(2)}, u32[]{:S(2)}) %collective-permute-start.8) | collective-permute-done | bytes 524320 | tf_op jit(solution)/shard_map/ppermute | solution.py:16
  38.2 2.9 %collective-permute-start.5 = (f32[64,256]{1,0:T(8,128)S(1)}, f32[64,256]{1,0:T(8,128)S(1)}, u32[]{:S(2)}, u32[]{:S(2)}) collective-permute-start(f32[64,256]{1,0:T(8,128)S(1)} %add.124), channel_id=1, source_target_pairs={{0,16},{4,20},{8,24},{12,28},{16,0},{20,4},{24,8},{28,12},{1,17},{... | collective-permute-start | bytes 196616 | tf_op jit(solution)/shard_map/ppermute | solution.py:16
  41.0 0.9 constant_dynamic-slice_fusion.2
  41.9 1.5 collective-permute-start.20
  43.4 1.6 %collective-permute-done.5 = f32[64,256]{1,0:T(8,128)S(1)} collective-permute-done((f32[64,256]{1,0:T(8,128)S(1)}, f32[64,256]{1,0:T(8,128)S(1)}, u32[]{:S(2)}, u32[]{:S(2)}) %collective-permute-start.5) | collective-permute-done | bytes 65568 | tf_op jit(solution)/shard_map/ppermute | solution.py:16
  45.1 1.6 %collective-permute-start.6 = (f32[64,256]{1,0:T(8,128)S(1)}, f32[64,256]{1,0:T(8,128)S(1)}, u32[]{:S(2)}, u32[]{:S(2)}) collective-permute-start(f32[64,256]{1,0:T(8,128)S(1)} %add.125), channel_id=1, source_target_pairs={{0,2},{1,3},{2,0},{3,1},{4,6},{5,7},{6,4},{7,5},{8,10},{9,11},{10,... | collective-permute-start | bytes 196616 | tf_op jit(solution)/shard_map/ppermute | solution.py:16
  46.7 1.3 maximum_select_fusion.1
  48.0 1.8 %fusion.22 = f32[256,256]{1,0:T(8,128)S(1)} fusion(f32[1024,256]{1,0:T(8,128)S(1)} %maximum_select_fusion.1, f32[1024,256]{1,0:T(8,128)S(1)} %maximum_select_fusion), kind=kOutput, calls=%fused_computation.51 | convolution fusion | flops 805306368 | bytes 2359296 | tf_op jit(solution)/shard_map/dot_general | solution.py:41
  49.8 1.8 %fusion.23 = f32[256,256]{1,0:T(8,128)S(1)} fusion(f32[1024,256]{1,0:T(8,128)S(1)} %maximum_select_fusion.1), kind=kOutput, calls=%fused_computation.52 | convolution fusion | flops 805306368 | bytes 1310720 | tf_op jit(solution)/shard_map/dot_general | solution.py:41
  51.7 3.0 %fusion.18 = f32[256,1024]{1,0:T(8,128)S(1)} fusion(f32[1024,256]{1,0:T(8,128)S(1)} %maximum_select_fusion.1, f32[1024,1024]{1,0:T(8,128)S(1)} %copy-done.1, f32[128,8,8,128]{3,2,1,0:T(8,128)S(1)} %bitcast.31), kind=kOutput, calls=%fused_computation.47 | convolution fusion | flops 1611661312 | bytes 10485760 | tf_op jit(solution)/shard_map/dot_general | solution.py:41
  54.7 0.9 constant_dynamic-slice_fusion.6
  56.4 1.6 %collective-permute-start.11 = (f32[64,512]{1,0:T(8,128)S(1)}, f32[64,512]{1,0:T(8,128)S(1)}, u32[]{:S(2)}, u32[]{:S(2)}) collective-permute-start(f32[64,512]{1,0:T(8,128)S(1)} %pad_maximum_fusion.1), channel_id=1, source_target_pairs={{0,4},{4,0},{8,12},{12,8},{16,20},{20,16},{24,28},{28,24},{1,5},{5... | collective-permute-start | bytes 393224 | tf_op jit(solution)/shard_map/ppermute | solution.py:16
  58.0 7.4 %shard_map.60 = (f32[128,128]{1,0:T(8,128)}, f32[128,128]{1,0:T(8,128)}, f32[128,128]{1,0:T(8,128)}, f32[128,128]{1,0:T(8,128)}) custom-call(f32[128,256]{1,0:T(8,128)} %copy-done.10, f32[128,256]{1,0:T(8,128)} %collective-permute-done.10.refs_1_), custom_call_target="tpu_custom_call" | custom-call | tf_op jit(solution)/shard_map/pallas_call | solution.py:203
  65.4 1.1 add.142
  66.5 1.4 collective-permute-start.12
  67.9 0.8 collective-permute-start.21
  68.7 7.0 %shard_map.61 = (f32[128,128]{1,0:T(8,128)}, f32[128,256]{1,0:T(8,128)}) custom-call(f32[128,128]{1,0:T(8,128)} %get-tuple-element.46.refs_0_, f32[128,128]{1,0:T(8,128)} %get-tuple-element.47.refs_1_), custom_call_target="tpu_custom_call" | custom-call | tf_op jit(solution)/shard_map/pallas_call | solution.py:203
  75.7 3.4 %collective-permute-start.13 = (f32[64,512]{1,0:T(8,128)S(1)}, f32[64,512]{1,0:T(8,128)S(1)}, u32[]{:S(2)}, u32[]{:S(2)}) collective-permute-start(f32[64,512]{1,0:T(8,128)S(1)} %add.129), channel_id=1, source_target_pairs={{0,16},{4,20},{8,24},{12,28},{16,0},{20,4},{24,8},{28,12},{1,17},{... | collective-permute-start | bytes 393224 | tf_op jit(solution)/shard_map/ppermute | solution.py:16
  79.1 6.1 %collective-permute-done.13 = f32[64,512]{1,0:T(8,128)S(1)} collective-permute-done((f32[64,512]{1,0:T(8,128)S(1)}, f32[64,512]{1,0:T(8,128)S(1)}, u32[]{:S(2)}, u32[]{:S(2)}) %collective-permute-start.13) | collective-permute-done | bytes 131104 | tf_op jit(solution)/shard_map/ppermute | solution.py:16
  85.8 1.0 add.145
  86.9 1.1 add.135
  88.0 1.5 collective-permute-start.17
  89.5 0.9 collective-permute-done.14
  90.4 1.0 maximum_select_fusion.9.refs_0_
  91.5 8.7 %collective-permute-done.22 = f32[64,1024]{1,0:T(8,128)} collective-permute-done((f32[64,1024]{1,0:T(8,128)S(1)}, f32[64,1024]{1,0:T(8,128)}, u32[]{:S(2)}, u32[]{:S(2)}) %collective-permute-start.22) | collective-permute-done | bytes 262176 | tf_op jit(solution)/shard_map/ppermute | solution.py:16
  100.1 1.0 add.146
  101.2 1.0 add.138
  102.2 2.5 %collective-permute-start.18 = (f32[64,1024]{1,0:T(8,128)S(1)}, f32[64,1024]{1,0:T(8,128)S(1)}, u32[]{:S(2)}, u32[]{:S(2)}) collective-permute-start(f32[64,1024]{1,0:T(8,128)S(1)} %add.138), channel_id=1, source_target_pairs={{0,16},{4,20},{8,24},{12,28},{16,0},{20,4},{24,8},{28,12},{1,17},{... | collective-permute-start | bytes 786440 | tf_op jit(solution)/shard_map/ppermute | solution.py:16
  104.7 9.0 %shard_map.62 = (f32[128,128]{1,0:T(8,128)}, f32[128,384]{1,0:T(8,128)}, f32[128,128]{1,0:T(8,128)}, f32[128,384]{1,0:T(8,128)}) custom-call(f32[128,512]{1,0:T(8,128)} %copy-done.9, f32[128,512]{1,0:T(8,128)} %collective-permute-done.15.refs_1_, f32[128,128]{1,0:T(8,128)} %get-tuple-element.50.refs_2_, f32[128,256]{1,0:T(8,128)} %get-tuple-element.51.refs_3_), custom_call_target="tpu_custom_call" | custom-call | tf_op jit(solution)/shard_map/pallas_call | solution.py:203
  113.8 7.9 %shard_map.63 = (f32[128,128]{1,0:T(8,128)}, f32[512,512]{1,0:T(8,128)}) custom-call(f32[128,128]{1,0:T(8,128)} %get-tuple-element.53.refs_0_, f32[128,384]{1,0:T(8,128)} %get-tuple-element.54.refs_1_, f32[128,128]{1,0:T(8,128)} %get-tuple-element.50.refs_2_, f32[128,256]{1,0:T(8,128)} %get-tuple-element.51.refs_3_, f32[128,384]{1,0:T(8,128)} %get-tuple-element.55.refs_4_), custom_call_target="tpu_custom_call" | custom-call | tf_op jit(solution)/shard_map/pallas_call | solution.py:203
  121.6 1.7 %fusion.10 = f32[1024,256]{1,0:T(8,128)S(1)} fusion(f32[1024,256]{1,0:T(8,128)S(1)} %maximum_select_fusion.1, f32[512,512]{1,0:T(8,128)} %get-tuple-element.62), kind=kOutput, calls=%fused_computation.25 | convolution fusion | flops 402653184 | bytes 2359296 | tf_op jit(solution)/shard_map/dot_general | solution.py:45
  123.4 1.5 collective-permute-start.19
  125.6 7.0 %collective-permute-done.19 = f32[64,1024]{1,0:T(8,128)S(1)} collective-permute-done((f32[64,1024]{1,0:T(8,128)S(1)}, f32[64,1024]{1,0:T(8,128)S(1)}, u32[]{:S(2)}, u32[]{:S(2)}) %collective-permute-start.19) | collective-permute-done | bytes 262176 | tf_op jit(solution)/shard_map/ppermute | solution.py:16
  133.4 9.0 %collective-permute-done.24 = f32[128,1024]{1,0:T(8,128)S(1)} collective-permute-done((f32[128,1024]{1,0:T(8,128)S(1)}, f32[128,1024]{1,0:T(8,128)S(1)}, u32[]{:S(2)}, u32[]{:S(2)}) %collective-permute-start.24) | collective-permute-done | bytes 524320 | tf_op jit(solution)/shard_map/ppermute | solution.py:16
  143.1 2.5 %convolution_subtract_fusion.1 = f32[1024,1024]{1,0:T(8,128)S(1)} fusion(f32[1024,256]{1,0:T(8,128)S(1)} %fusion.24, f32[256,1024]{1,0:T(8,128)S(1)} %fusion.6, f32[1024,1024]{1,0:T(8,128)S(1)} %copy-done.2, f32[128,8,8,128]{3,2,1,0:T(8,128)S(1)} %bitcast.32), kind=kOutput, calls=%fused_computation.2 | convolution fusion | flops 1612709888 | bytes 14680064 | tf_op jit(solution)/shard_map/dot_general | solution.py:305
  145.8 0.7 pad_maximum_fusion
  148.5 3.8 %convolution_subtract_fusion = f32[1024,1024]{1,0:T(8,128)} fusion(f32[1024,1024]{1,0:T(8,128)S(1)} %convolution_subtract_fusion.1, f32[1024,256]{1,0:T(8,128)S(1)} %convolution_add_fusion, f32[256,1024]{1,0:T(8,128)S(1)} %get-tuple-element.82), kind=kOutput, calls=%fused_computation.1 | convolution fusion | flops 1611661312 | bytes 10485760 | tf_op jit(solution)/shard_map/dot_general | solution.py:307
  (89 shorter events, 7.6 us)
Async XLA Ops:
  3.5 3.5 %copy-start.7 = (f32[1024,256]{1,0:T(8,128)S(1)}, f32[1024,256]{1,0:T(8,128)}, u32[]{:S(2)}) copy-start(f32[1024,256]{1,0:T(8,128)} %shard_map.58) | copy-start | bytes 3145732
  3.5 18.9 %copy-start.15 = (s32[8,8]{1,0:T(8,128)S(1)}, s32[8,8]{1,0:T(8,128)}, u32[]{:S(2)}) copy-start(s32[8,8]{1,0:T(8,128)} %refs_1_.3) | copy-start | bytes 772
  3.5 3.5 %collective-permute-start = (f32[1024,256]{1,0:T(8,128)}, f32[1024,256]{1,0:T(8,128)S(1)}, u32[]{:S(2)}, u32[]{:S(2)}) collective-permute-start(f32[1024,256]{1,0:T(8,128)} %shard_map.58), channel_id=1, source_target_pairs={{0,1},{1,0},{2,3},{3,2},{4,5},{5,4},{6,7},{7,6},{8,9},{9,8},{10,11... | collective-permute-start | bytes 3145736 | tf_op jit(solution)/shard_map/ppermute | solution.py:16
  6.9 15.6 %collective-permute-start.7 = (f32[1024,256]{1,0:T(8,128)}, f32[1024,256]{1,0:T(8,128)S(1)}, u32[]{:S(2)}, u32[]{:S(2)}) collective-permute-start(f32[1024,256]{1,0:T(8,128)} %shard_map.59), channel_id=1, source_target_pairs={{0,1},{1,0},{2,3},{3,2},{4,5},{5,4},{6,7},{7,6},{8,9},{9,8},{10,11... | collective-permute-start | bytes 3145736 | tf_op jit(solution)/shard_map/ppermute | solution.py:16
  7.1 15.2 %collective-permute-start.1 = (f32[1024,128]{1,0:T(8,128)S(1)}, f32[1024,128]{1,0:T(8,128)S(1)}, u32[]{:S(2)}, u32[]{:S(2)}) collective-permute-start(f32[1024,128]{1,0:T(8,128)S(1)} %dynamic-slice_add_fusion.1), channel_id=1, source_target_pairs={{0,2},{1,3},{2,0},{3,1},{4,6},{5,7},{6,4},{7,5},{8,10},{9,11},{10,... | collective-permute-start | bytes 1572872 | tf_op jit(solution)/shard_map/ppermute | solution.py:16
  22.3 3.1 %collective-permute-start.2 = (f32[1024,128]{1,0:T(8,128)S(1)}, f32[1024,128]{1,0:T(8,128)S(1)}, u32[]{:S(2)}, u32[]{:S(2)}) collective-permute-start(f32[1024,128]{1,0:T(8,128)S(1)} %add.120), channel_id=1, source_target_pairs={{0,1},{1,0},{2,3},{3,2},{4,5},{5,4},{6,7},{7,6},{8,9},{9,8},{10,11... | collective-permute-start | bytes 1572872 | tf_op jit(solution)/shard_map/ppermute | solution.py:16
  23.6 5.7 %copy-start = (f32[1024,1024]{1,0:T(8,128)S(1)}, f32[1024,1024]{1,0:T(8,128)}, u32[]{:S(2)}) copy-start(f32[1024,1024]{1,0:T(8,128)} %refs_2_.3) | copy-start | bytes 12582916
  23.6 14.4 %collective-permute-start.8 = (f32[1024,128]{1,0:T(8,128)S(1)}, f32[1024,128]{1,0:T(8,128)S(1)}, u32[]{:S(2)}, u32[]{:S(2)}) collective-permute-start(f32[1024,128]{1,0:T(8,128)S(1)} %dynamic-slice_add_fusion), channel_id=1, source_target_pairs={{0,2},{1,3},{2,0},{3,1},{4,6},{5,7},{6,4},{7,5},{8,10},{9,11},{10,... | collective-permute-start | bytes 1572872 | tf_op jit(solution)/shard_map/ppermute | solution.py:16
  27.3 4.7 %collective-permute-start.3 = (f32[64,256]{1,0:T(8,128)S(1)}, f32[64,256]{1,0:T(8,128)S(1)}, u32[]{:S(2)}, u32[]{:S(2)}) collective-permute-start(f32[64,256]{1,0:T(8,128)S(1)} %constant_dynamic-slice_fusion.10), channel_id=1, source_target_pairs={{0,4},{4,0},{8,12},{12,8},{16,20},{20,16},{24,28},{28,24},{1,5},{5... | collective-permute-start | bytes 196616 | tf_op jit(solution)/shard_map/ppermute | solution.py:16
  29.2 2.8 %copy-start.3 = (f32[8,128,8,128]{3,2,1,0:T(8,128)}, f32[8,128,8,128]{3,2,1,0:T(8,128)S(1)}, u32[]{:S(2)}) copy-start(f32[8,128,8,128]{3,2,1,0:T(8,128)S(1)} %mul.50) | copy-start | bytes 12582916
  32.1 4.3 %collective-permute-start.4 = (f32[64,256]{1,0:T(8,128)S(1)}, f32[64,256]{1,0:T(8,128)S(1)}, u32[]{:S(2)}, u32[]{:S(2)}) collective-permute-start(f32[64,256]{1,0:T(8,128)S(1)} %add.123), channel_id=1, source_target_pairs={{0,8},{4,12},{8,0},{12,4},{16,24},{20,28},{24,16},{28,20},{1,9},{5... | collective-permute-start | bytes 196616 | tf_op jit(solution)/shard_map/ppermute | solution.py:16
  38.0 8.7 %collective-permute-start.9 = (f32[1024,128]{1,0:T(8,128)S(1)}, f32[1024,128]{1,0:T(8,128)}, u32[]{:S(2)}, u32[]{:S(2)}) collective-permute-start(f32[1024,128]{1,0:T(8,128)S(1)} %add.127), channel_id=1, source_target_pairs={{0,1},{1,0},{2,3},{3,2},{4,5},{5,4},{6,7},{7,6},{8,9},{9,8},{10,11... | collective-permute-start | bytes 1572872 | tf_op jit(solution)/shard_map/ppermute | solution.py:16
  38.2 6.9 %collective-permute-start.5 = (f32[64,256]{1,0:T(8,128)S(1)}, f32[64,256]{1,0:T(8,128)S(1)}, u32[]{:S(2)}, u32[]{:S(2)}) collective-permute-start(f32[64,256]{1,0:T(8,128)S(1)} %add.124), channel_id=1, source_target_pairs={{0,16},{4,20},{8,24},{12,28},{16,0},{20,4},{24,8},{28,12},{1,17},{... | collective-permute-start | bytes 196616 | tf_op jit(solution)/shard_map/ppermute | solution.py:16
  41.0 10.7 %copy-start.4 = (f32[8,128,8,128]{3,2,1,0:T(8,128)S(1)}, f32[8,128,8,128]{3,2,1,0:T(8,128)}, u32[]{:S(2)}) copy-start(f32[8,128,8,128]{3,2,1,0:T(8,128)} %copy-done.3) | copy-start | bytes 12582916
  41.9 9.8 %copy-start.1 = (f32[1024,1024]{1,0:T(8,128)S(1)}, f32[1024,1024]{1,0:T(8,128)}, u32[]{:S(2)}) copy-start(f32[1024,1024]{1,0:T(8,128)} %refs_2_.3) | copy-start | bytes 12582916
  41.9 23.4 %collective-permute-start.20 = (f32[128,1024]{1,0:T(8,128)}, f32[128,1024]{1,0:T(8,128)}, u32[]{:S(2)}, u32[]{:S(2)}) collective-permute-start(f32[128,1024]{1,0:T(8,128)} %get-tuple-element.73), channel_id=1, source_target_pairs={{0,4},{4,0},{8,12},{12,8},{16,20},{20,16},{24,28},{28,24},{1,5},{5... | collective-permute-start | bytes 1572872 | tf_op jit(solution)/shard_map/ppermute | solution.py:16
  45.1 11.2 %collective-permute-start.6 = (f32[64,256]{1,0:T(8,128)S(1)}, f32[64,256]{1,0:T(8,128)S(1)}, u32[]{:S(2)}, u32[]{:S(2)}) collective-permute-start(f32[64,256]{1,0:T(8,128)S(1)} %add.125), channel_id=1, source_target_pairs={{0,2},{1,3},{2,0},{3,1},{4,6},{5,7},{6,4},{7,5},{8,10},{9,11},{10,... | collective-permute-start | bytes 196616 | tf_op jit(solution)/shard_map/ppermute | solution.py:16
  55.6 31.3 %collective-permute-start.16 = (f32[128,1024]{1,0:T(8,128)}, f32[128,1024]{1,0:T(8,128)}, u32[]{:S(2)}, u32[]{:S(2)}) collective-permute-start(f32[128,1024]{1,0:T(8,128)} %get-tuple-element.75), channel_id=1, source_target_pairs={{0,8},{4,12},{8,0},{12,4},{16,24},{20,28},{24,16},{28,20},{1,9},{5... | collective-permute-start | bytes 1572872 | tf_op jit(solution)/shard_map/ppermute | solution.py:16
  56.3 1.7 %copy-start.10 = (f32[128,256]{1,0:T(8,128)}, f32[128,256]{1,0:T(8,128)S(1)}, u32[]{:S(2)}) copy-start(f32[128,256]{1,0:T(8,128)S(1)} %maximum_select_fusion.10.refs_0_) | copy-start | bytes 393220
  56.3 1.6 %collective-permute-start.10 = (f32[128,256]{1,0:T(8,128)S(1)}, f32[128,256]{1,0:T(8,128)}, u32[]{:S(2)}, u32[]{:S(2)}) collective-permute-start(f32[128,256]{1,0:T(8,128)S(1)} %maximum_select_fusion.10.refs_0_), channel_id=1, source_target_pairs={{0,1},{1,0},{2,3},{3,2},{4,5},{5,4},{6,7},{7,6},{8,9},{9,8},{10,11... | collective-permute-start | bytes 393224 | tf_op jit(solution)/shard_map/ppermute | solution.py:16
  56.4 10.1 %collective-permute-start.11 = (f32[64,512]{1,0:T(8,128)S(1)}, f32[64,512]{1,0:T(8,128)S(1)}, u32[]{:S(2)}, u32[]{:S(2)}) collective-permute-start(f32[64,512]{1,0:T(8,128)S(1)} %pad_maximum_fusion.1), channel_id=1, source_target_pairs={{0,4},{4,0},{8,12},{12,8},{16,20},{20,16},{24,28},{28,24},{1,5},{5... | collective-permute-start | bytes 393224 | tf_op jit(solution)/shard_map/ppermute | solution.py:16
  66.5 9.2 %collective-permute-start.12 = (f32[64,512]{1,0:T(8,128)S(1)}, f32[64,512]{1,0:T(8,128)S(1)}, u32[]{:S(2)}, u32[]{:S(2)}) collective-permute-start(f32[64,512]{1,0:T(8,128)S(1)} %add.128), channel_id=1, source_target_pairs={{0,8},{4,12},{8,0},{12,4},{16,24},{20,28},{24,16},{28,20},{1,9},{5... | collective-permute-start | bytes 393224 | tf_op jit(solution)/shard_map/ppermute | solution.py:16
  67.9 17.8 %collective-permute-start.21 = (f32[64,1024]{1,0:T(8,128)S(1)}, f32[64,1024]{1,0:T(8,128)}, u32[]{:S(2)}, u32[]{:S(2)}) collective-permute-start(f32[64,1024]{1,0:T(8,128)S(1)} %get-tuple-element.77), channel_id=1, source_target_pairs={{0,8},{4,12},{8,0},{12,4},{16,24},{20,28},{24,16},{28,20},{1,9},{5... | collective-permute-start | bytes 786440 | tf_op jit(solution)/shard_map/ppermute | solution.py:16
  75.7 9.5 %collective-permute-start.13 = (f32[64,512]{1,0:T(8,128)S(1)}, f32[64,512]{1,0:T(8,128)S(1)}, u32[]{:S(2)}, u32[]{:S(2)}) collective-permute-start(f32[64,512]{1,0:T(8,128)S(1)} %add.129), channel_id=1, source_target_pairs={{0,16},{4,20},{8,24},{12,28},{16,0},{20,4},{24,8},{28,12},{1,17},{... | collective-permute-start | bytes 393224 | tf_op jit(solution)/shard_map/ppermute | solution.py:16
  85.2 5.1 %collective-permute-start.14 = (f32[64,512]{1,0:T(8,128)S(1)}, f32[64,512]{1,0:T(8,128)}, u32[]{:S(2)}, u32[]{:S(2)}) collective-permute-start(f32[64,512]{1,0:T(8,128)S(1)} %add.130), channel_id=1, source_target_pairs={{0,2},{1,3},{2,0},{3,1},{4,6},{5,7},{6,4},{7,5},{8,10},{9,11},{10,... | collective-permute-start | bytes 393224 | tf_op jit(solution)/shard_map/ppermute | solution.py:16
  86.8 13.4 %collective-permute-start.22 = (f32[64,1024]{1,0:T(8,128)S(1)}, f32[64,1024]{1,0:T(8,128)}, u32[]{:S(2)}, u32[]{:S(2)}) collective-permute-start(f32[64,1024]{1,0:T(8,128)S(1)} %add.145), channel_id=1, source_target_pairs={{0,16},{4,20},{8,24},{12,28},{16,0},{20,4},{24,8},{28,12},{1,17},{... | collective-permute-start | bytes 786440 | tf_op jit(solution)/shard_map/ppermute | solution.py:16
  88.0 13.2 %collective-permute-start.17 = (f32[64,1024]{1,0:T(8,128)S(1)}, f32[64,1024]{1,0:T(8,128)}, u32[]{:S(2)}, u32[]{:S(2)}) collective-permute-start(f32[64,1024]{1,0:T(8,128)S(1)} %get-tuple-element.79), channel_id=1, source_target_pairs={{0,4},{4,0},{8,12},{12,8},{16,20},{20,16},{24,28},{28,24},{1,5},{5... | collective-permute-start | bytes 786440 | tf_op jit(solution)/shard_map/ppermute | solution.py:16
  91.4 13.4 %copy-start.9 = (f32[128,512]{1,0:T(8,128)}, f32[128,512]{1,0:T(8,128)S(1)}, u32[]{:S(2)}) copy-start(f32[128,512]{1,0:T(8,128)S(1)} %maximum_select_fusion.9.refs_0_) | copy-start | bytes 786436
  91.4 13.4 %collective-permute-start.15 = (f32[128,512]{1,0:T(8,128)S(1)}, f32[128,512]{1,0:T(8,128)}, u32[]{:S(2)}, u32[]{:S(2)}) collective-permute-start(f32[128,512]{1,0:T(8,128)S(1)} %maximum_select_fusion.9.refs_0_), channel_id=1, source_target_pairs={{0,1},{1,0},{2,3},{3,2},{4,5},{5,4},{6,7},{7,6},{8,9},{9,8},{10,11... | collective-permute-start | bytes 786440 | tf_op jit(solution)/shard_map/ppermute | solution.py:16
  101.1 23.7 %collective-permute-start.23 = (f32[64,1024]{1,0:T(8,128)S(1)}, f32[64,1024]{1,0:T(8,128)S(1)}, u32[]{:S(2)}, u32[]{:S(2)}) collective-permute-start(f32[64,1024]{1,0:T(8,128)S(1)} %add.146), channel_id=1, source_target_pairs={{0,8},{4,12},{8,0},{12,4},{16,24},{20,28},{24,16},{28,20},{1,9},{5... | collective-permute-start | bytes 786440 | tf_op jit(solution)/shard_map/ppermute | solution.py:16
  102.2 21.1 %collective-permute-start.18 = (f32[64,1024]{1,0:T(8,128)S(1)}, f32[64,1024]{1,0:T(8,128)S(1)}, u32[]{:S(2)}, u32[]{:S(2)}) collective-permute-start(f32[64,1024]{1,0:T(8,128)S(1)} %add.138), channel_id=1, source_target_pairs={{0,16},{4,20},{8,24},{12,28},{16,0},{20,4},{24,8},{28,12},{1,17},{... | collective-permute-start | bytes 786440 | tf_op jit(solution)/shard_map/ppermute | solution.py:16
  121.6 4.0 %copy-start.6 = (f32[512,512]{1,0:T(8,128)S(1)}, f32[512,512]{1,0:T(8,128)}, u32[]{:S(2)}) copy-start(f32[512,512]{1,0:T(8,128)} %get-tuple-element.62) | copy-start | bytes 3145732
  123.3 19.7 %copy-start.2 = (f32[1024,1024]{1,0:T(8,128)S(1)}, f32[1024,1024]{1,0:T(8,128)}, u32[]{:S(2)}) copy-start(f32[1024,1024]{1,0:T(8,128)} %refs_2_.3) | copy-start | bytes 12582916
  123.3 19.7 %copy-start.5 = (f32[8,128,8,128]{3,2,1,0:T(8,128)S(1)}, f32[8,128,8,128]{3,2,1,0:T(8,128)}, u32[]{:S(2)}) copy-start(f32[8,128,8,128]{3,2,1,0:T(8,128)} %copy-done.3) | copy-start | bytes 12582916
  123.4 9.2 %collective-permute-start.19 = (f32[64,1024]{1,0:T(8,128)S(1)}, f32[64,1024]{1,0:T(8,128)S(1)}, u32[]{:S(2)}, u32[]{:S(2)}) collective-permute-start(f32[64,1024]{1,0:T(8,128)S(1)} %add.139), channel_id=1, source_target_pairs={{0,4},{4,0},{8,12},{12,8},{16,20},{20,16},{24,28},{28,24},{1,5},{5... | collective-permute-start | bytes 786440 | tf_op jit(solution)/shard_map/ppermute | solution.py:16
  124.9 17.5 %collective-permute-start.24 = (f32[128,1024]{1,0:T(8,128)S(1)}, f32[128,1024]{1,0:T(8,128)S(1)}, u32[]{:S(2)}, u32[]{:S(2)}) collective-permute-start(f32[128,1024]{1,0:T(8,128)S(1)} %maximum_select_fusion.8), channel_id=1, source_target_pairs={{0,4},{4,0},{8,12},{12,8},{16,20},{20,16},{24,28},{28,24},{1,5},{5... | collective-permute-start | bytes 1572872 | tf_op jit(solution)/shard_map/ppermute | solution.py:16
  132.7 14.5 %collective-permute-start.25 = (f32[128,1024]{1,0:T(8,128)S(1)}, f32[128,1024]{1,0:T(8,128)S(1)}, u32[]{:S(2)}, u32[]{:S(2)}) collective-permute-start(f32[128,1024]{1,0:T(8,128)S(1)} %maximum_select_fusion.7), channel_id=1, source_target_pairs={{0,8},{4,12},{8,0},{12,4},{16,24},{20,28},{24,16},{28,20},{1,9},{5... | collective-permute-start | bytes 1572872 | tf_op jit(solution)/shard_map/ppermute | solution.py:16
  143.0 2.8 %copy-start.11 = (f32[128,128]{1,0:T(8,128)S(1)}, f32[128,128]{1,0:T(8,128)}, u32[]{:S(2)}) copy-start(f32[128,128]{1,0:T(8,128)} %get-tuple-element.43) | copy-start | bytes 196612
  143.0 2.8 %copy-start.12 = (f32[128,128]{1,0:T(8,128)S(1)}, f32[128,128]{1,0:T(8,128)}, u32[]{:S(2)}) copy-start(f32[128,128]{1,0:T(8,128)} %get-tuple-element.48) | copy-start | bytes 196612
  143.0 2.8 %copy-start.13 = (f32[128,128]{1,0:T(8,128)S(1)}, f32[128,128]{1,0:T(8,128)}, u32[]{:S(2)}) copy-start(f32[128,128]{1,0:T(8,128)} %get-tuple-element.52) | copy-start | bytes 196612
  143.1 2.8 %copy-start.14 = (f32[128,128]{1,0:T(8,128)S(1)}, f32[128,128]{1,0:T(8,128)}, u32[]{:S(2)}) copy-start(f32[128,128]{1,0:T(8,128)} %get-tuple-element.61) | copy-start | bytes 196612
  148.5 3.9 %copy-start.8 = (f32[512,1024]{1,0:T(8,128)}, f32[512,1024]{1,0:T(8,128)S(1)}, u32[]{:S(2)}) copy-start(f32[512,1024]{1,0:T(8,128)S(1)} %get-tuple-element.81) | copy-start | bytes 6291460
